TPU v7x, 32 devices: a whole 2x2x4 slice. The times are simulated.
32 devices in a mesh: ray: 4 (over z), cell: 8 (over y, x, core).
Axes of the slice: x: 2, y: 2, z: 4, core: 2. Of those that a mesh axis runs over, the one named last changes fastest.
Arguments:
- right_side: float32 [8, 8192], P(None, 'ray'), may hold values from -6 to 6
- tiles: bfloat16 [32, 32, 256, 256], P('ray', 'cell'), may hold values from -0.375 to 0.375
- pattern: int32 [32, 32], P('ray', 'cell'), may hold values from 0 to 31, as said below
- counts: int32 [32, 8], P('ray', 'cell'), may hold values from 1 to 4, as said below
Outputs:
- solution: float32 [8, 65536], P(None, 'cell')
- misfit: float32 [8], replicated
Inputs may be any that keep to these rules, and one draw needn't show every extreme that they name: `pattern`: each entry indexes a block within the slot's group of 32 cell blocks; a bundle may name a block more than once. Ragged counts; some bundle has all 4 slots live in some group, and some has one.
All inputs are finite; a program needn't handle non-finite values.
Results may differ from a plain program's by a relative error of at most 0.0014.
Values may be sent and summed in bfloat16 or wider, within the bound.
A program may use at most 64 MiB of HBM per device.

v0:
```python
import jax
import jax.numpy as jnp
from jax import lax
from jax.sharding import PartitionSpec as P

BLK_DEV = 32
ITERS = 4


def norm_rows(local_sq):
    total = lax.psum(local_sq, "ray")
    return jnp.sqrt(total + 1e-06)


def norm_cols(local_sq):
    total = lax.psum(local_sq, "cell")
    return jnp.sqrt(total + 1e-06)


def local(right_side, tiles, pattern, counts):
    nrhs = right_side.shape[0]
    bundles = tiles.shape[0]
    slots = tiles.shape[1]
    ray_rows = tiles.shape[2]
    block_cells = tiles.shape[3]
    blocks = BLK_DEV
    live = lax.broadcasted_iota(jnp.int32, pattern.shape, 1) < counts
    live_bf = live.astype(jnp.bfloat16)
    selector = (
        (pattern[:, :, None] == lax.broadcasted_iota(jnp.int32, (bundles, slots, blocks), 2))
        & live[:, :, None]
    ).astype(jnp.float32)

    def adjoint(vector_bf):
        rows = vector_bf.reshape(nrhs, bundles, ray_rows)
        per = jnp.einsum("bsrc,nbr->bsnc", tiles, rows, preferred_element_type=jnp.float32)
        total = jnp.einsum("bsk,bsnc->nkc", selector, per, precision=lax.Precision.HIGHEST)
        return total.reshape(nrhs, blocks * block_cells)

    u_state = right_side
    beta = norm_rows(jnp.sum(u_state * u_state, axis=1))
    u_state = u_state / beta[:, None]

    def rows_bf(state):
        return state.astype(jnp.bfloat16)

    def cols_reduce(adj_terms):
        return lax.psum(adj_terms, "ray")

    v_state = cols_reduce(adjoint(rows_bf(u_state)))
    alpha = norm_cols(jnp.sum(v_state * v_state, axis=1))
    v_state = v_state / alpha[:, None]
    w_state = v_state
    x_state = jnp.zeros_like(v_state)
    phibar = beta
    rhobar = alpha
    for step in range(ITERS):
        vblocks = v_state.astype(jnp.bfloat16).reshape(nrhs, blocks, block_cells)
        picked = vblocks[:, pattern] * live_bf[None, :, :, None]
        partial_value = jnp.einsum(
            "bsrc,nbsc->nbr", tiles, picked, preferred_element_type=jnp.float32
        )
        partial_value = partial_value.reshape(nrhs, bundles * ray_rows)
        summed = lax.psum(partial_value, "cell")
        u_state = summed - alpha[:, None] * u_state
        beta = norm_rows(jnp.sum(u_state * u_state, axis=1))
        u_state = u_state / beta[:, None]
        v_state = cols_reduce(adjoint(rows_bf(u_state))) - beta[:, None] * v_state
        alpha = norm_cols(jnp.sum(v_state * v_state, axis=1))
        v_state = v_state / alpha[:, None]
        rho = jnp.sqrt(rhobar * rhobar + beta * beta)
        cosine = rhobar / rho
        sine = beta / rho
        theta = sine * alpha
        rhobar = -cosine * alpha
        phi = cosine * phibar
        phibar = sine * phibar
        x_state = x_state + (phi / rho)[:, None] * w_state
        w_state = v_state - (theta / rho)[:, None] * w_state
    return (x_state, phibar)


def solution(mesh):
    in_specs = (P(None, "ray"), P("ray", "cell", None, None), P("ray", "cell"), P("ray", "cell"))
    out_specs = (P(None, "cell"), P())
    return jax.shard_map(local, mesh=mesh, in_specs=in_specs, out_specs=out_specs, check_vma=False)
```

profile of v0, /device:TPU:0, one launch (start us, length us, event | category | flops | bytes accessed | tf_op | source)
XLA Modules:
  0.0 515.1 jit_solution(9101913132747717034)
XLA Ops:
  7.2 1.0 multiply_reduce_fusion.8
  8.2 13.5 %psum.119 = f32[8]{0:T(128)S(1)} all-reduce(f32[8]{0:T(128)S(1)} %multiply_reduce_fusion.8), channel_id=1, replica_groups=mesh['ray'=4,'cell'=8] {'ray'}, use_global_device_ids=true, to_apply=%region_1.0 | all-reduce | flops 8 | bytes 64 | tf_op jit(solution)/shard_map/psum | solution.py:11
  21.7 0.7 fusion.33
  22.4 0.1 copy.8
  22.5 0.9 fusion.27
  23.4 2.8 fusion.51
  26.3 0.5 convolution_bitcast_fusion.3
  26.7 0.9 copy.26
  27.6 0.0 all-reduce.11.cloned.1.call-start
  27.7 0.1 copy.9
  27.8 0.1 reshape.127
  27.9 33.7 %all-reduce.9.cloned.1.call-done = f32[8,8192]{1,0:T(8,128)} async-done(((f32[8,8192]{1,0:T(8,128)}), f32[8,8192]{1,0:T(8,128)}) %all-reduce.9.cloned.1.call-update) | async-done | bytes 262160 | tf_op jit(solution)/shard_map/psum | solution.py:48
  61.6 1.1 multiply_reduce_fusion.3
  62.7 11.8 %psum.121 = f32[8]{0:T(128)S(1)} all-reduce(f32[8]{0:T(128)S(1)} %multiply_reduce_fusion.3), channel_id=1, replica_groups=mesh['ray'=4,'cell'=8] {'cell'}, use_global_device_ids=true, to_apply=%region_4.0 | all-reduce | flops 8 | bytes 64 | tf_op jit(solution)/shard_map/psum | solution.py:16
  74.5 1.0 fusion.42
  75.6 0.6 gather_fusion
  76.2 4.1 fusion.14
  80.3 52.3 %all-reduce.11.cloned.1.call-done = f32[8,2048]{1,0:T(8,128)} async-done(((f32[8,2048]{1,0:T(8,128)}), f32[8,2048]{1,0:T(8,128)}) %all-reduce.11.cloned.1.call-update) | async-done | bytes 65552 | tf_op jit(solution)/shard_map/psum | solution.py:64
  132.6 1.0 multiply_reduce_fusion.7
  133.6 11.7 %psum.123 = f32[8]{0:T(128)S(1)} all-reduce(f32[8]{0:T(128)S(1)} %get-tuple-element.21), channel_id=1, replica_groups=mesh['ray'=4,'cell'=8] {'ray'}, use_global_device_ids=true, to_apply=%region_7.0 | all-reduce | flops 8 | bytes 64 | tf_op jit(solution)/shard_map/psum | solution.py:11
  145.3 0.1 fusion.28
  145.4 2.8 fusion.52
  148.3 0.5 convolution_bitcast_fusion.2
  148.7 0.9 copy.27
  149.7 32.3 %all-reduce.13.cloned.1.call-done = f32[8,8192]{1,0:T(8,128)} async-done(((f32[8,8192]{1,0:T(8,128)}), f32[8,8192]{1,0:T(8,128)}) %all-reduce.13.cloned.1.call-update) | async-done | bytes 262160 | tf_op jit(solution)/shard_map/psum | solution.py:48
  182.0 1.2 multiply_reduce_fusion.2
  183.2 11.8 %psum.125 = f32[8]{0:T(128)S(1)} all-reduce(f32[8]{0:T(128)S(1)} %multiply_reduce_fusion.2), channel_id=1, replica_groups=mesh['ray'=4,'cell'=8] {'cell'}, use_global_device_ids=true, to_apply=%region_10.0 | all-reduce | flops 8 | bytes 64 | tf_op jit(solution)/shard_map/psum | solution.py:16
  195.0 1.1 fusion.50
  196.1 0.6 gather_fusion.1
  196.7 4.0 fusion.12
  200.7 0.0 all-reduce.17.cloned.1.call-start
  200.8 52.3 %all-reduce.15.cloned.1.call-done = f32[8,2048]{1,0:T(8,128)} async-done(((f32[8,2048]{1,0:T(8,128)}), f32[8,2048]{1,0:T(8,128)}) %all-reduce.15.cloned.1.call-update) | async-done | bytes 65552 | tf_op jit(solution)/shard_map/psum | solution.py:64
  253.0 1.0 multiply_reduce_fusion.6
  254.1 11.7 %psum.127 = f32[8]{0:T(128)S(1)} all-reduce(f32[8]{0:T(128)S(1)} %get-tuple-element.17), channel_id=1, replica_groups=mesh['ray'=4,'cell'=8] {'ray'}, use_global_device_ids=true, to_apply=%region_13.0 | all-reduce | flops 8 | bytes 64 | tf_op jit(solution)/shard_map/psum | solution.py:11
  265.8 0.1 fusion.29
  265.9 2.8 fusion.53
  268.7 0.5 convolution_bitcast_fusion.1
  269.2 0.9 copy.28
  270.1 32.3 %all-reduce.17.cloned.1.call-done = f32[8,8192]{1,0:T(8,128)} async-done(((f32[8,8192]{1,0:T(8,128)}), f32[8,8192]{1,0:T(8,128)}) %all-reduce.17.cloned.1.call-update) | async-done | bytes 262160 | tf_op jit(solution)/shard_map/psum | solution.py:48
  302.4 1.2 multiply_reduce_fusion.1
  303.6 11.8 %psum.129 = f32[8]{0:T(128)S(1)} all-reduce(f32[8]{0:T(128)S(1)} %multiply_reduce_fusion.1), channel_id=1, replica_groups=mesh['ray'=4,'cell'=8] {'cell'}, use_global_device_ids=true, to_apply=%region_16.0 | all-reduce | flops 8 | bytes 64 | tf_op jit(solution)/shard_map/psum | solution.py:16
  315.4 1.1 fusion.49
  316.5 0.6 gather_fusion.2
  317.1 4.0 fusion.10
  321.1 0.0 all-reduce.21.cloned.1.call-start
  321.2 52.3 %all-reduce.19.cloned.1.call-done = f32[8,2048]{1,0:T(8,128)} async-done(((f32[8,2048]{1,0:T(8,128)}), f32[8,2048]{1,0:T(8,128)}) %all-reduce.19.cloned.1.call-update) | async-done | bytes 65552 | tf_op jit(solution)/shard_map/psum | solution.py:64
  373.5 1.0 multiply_reduce_fusion.5
  374.5 11.7 %psum.131 = f32[8]{0:T(128)S(1)} all-reduce(f32[8]{0:T(128)S(1)} %get-tuple-element.13), channel_id=1, replica_groups=mesh['ray'=4,'cell'=8] {'ray'}, use_global_device_ids=true, to_apply=%region_19.0 | all-reduce | flops 8 | bytes 64 | tf_op jit(solution)/shard_map/psum | solution.py:11
  386.2 0.1 fusion.30
  386.3 2.8 fusion.54
  389.1 0.5 convolution_bitcast_fusion
  389.6 0.9 copy.29
  390.5 0.0 all-reduce.23.cloned.1.call-start
  390.5 32.3 %all-reduce.21.cloned.1.call-done = f32[8,8192]{1,0:T(8,128)} async-done(((f32[8,8192]{1,0:T(8,128)}), f32[8,8192]{1,0:T(8,128)}) %all-reduce.21.cloned.1.call-update) | async-done | bytes 262160 | tf_op jit(solution)/shard_map/psum | solution.py:48
  422.8 1.3 multiply_reduce_fusion
  424.1 11.8 %psum.133 = f32[8]{0:T(128)S(1)} all-reduce(f32[8]{0:T(128)S(1)} %multiply_reduce_fusion), channel_id=1, replica_groups=mesh['ray'=4,'cell'=8] {'cell'}, use_global_device_ids=true, to_apply=%region_22.0 | all-reduce | flops 8 | bytes 64 | tf_op jit(solution)/shard_map/psum | solution.py:16
  435.9 1.1 fusion.24
  437.0 0.6 gather_fusion.3
  437.6 4.0 fusion.8
  441.6 52.3 %all-reduce.23.cloned.1.call-done = f32[8,2048]{1,0:T(8,128)} async-done(((f32[8,2048]{1,0:T(8,128)}), f32[8,2048]{1,0:T(8,128)}) %all-reduce.23.cloned.1.call-update) | async-done | bytes 65552 | tf_op jit(solution)/shard_map/psum | solution.py:64
  493.9 1.0 multiply_reduce_fusion.4
  495.0 11.7 %psum.135 = f32[8]{0:T(128)S(1)} all-reduce(f32[8]{0:T(128)S(1)} %multiply_reduce_fusion.4), channel_id=1, replica_groups=mesh['ray'=4,'cell'=8] {'ray'}, use_global_device_ids=true, to_apply=%region_25.0 | all-reduce | flops 8 | bytes 64 | tf_op jit(solution)/shard_map/psum | solution.py:11
  506.7 0.6 divide_multiply_fusion
  507.3 0.9 multiply_add_fusion
  (31 shorter events, 0.4 us)
Async XLA Ops:
  7.2 19.1 %copy-start.3 = (s32[8,4]{0,1:T(4,128)S(1)}, s32[8,4]{0,1:T(4,128)}, u32[]{:S(2)}) copy-start(s32[8,4]{0,1:T(4,128)} %param.6) | copy-start | bytes 388
  7.2 54.4 %all-reduce.9.cloned.1.call-start = ((), (), s32[]{:S(2)}) async-start(), calls=%async_computation | async-start | bytes 524288 | tf_op jit(solution)/shard_map/psum | solution.py:48
  26.3 106.3 %copy-start.2 = (f32[8,2048]{1,0:T(8,128)S(1)}, f32[8,2048]{1,0:T(8,128)}, u32[]{:S(2)}) copy-start(f32[8,2048]{1,0:T(8,128)} %param.4) | copy-start | bytes 196612
  27.6 105.0 %all-reduce.11.cloned.1.call-start = ((), (), s32[]{:S(2)}) async-start(), calls=%async_computation.1 | async-start | bytes 131072 | tf_op jit(solution)/shard_map/psum | solution.py:64
  76.2 105.8 %copy-start = (f32[8,8192]{1,0:T(8,128)S(1)}, f32[8,8192]{1,0:T(8,128)}, u32[]{:S(2)}) copy-start(f32[8,8192]{1,0:T(8,128)} %all-reduce.9.cloned.1.call-done) | copy-start | bytes 786436
  80.3 101.7 %all-reduce.13.cloned.1.call-start = ((), (), s32[]{:S(2)}) async-start(), calls=%async_computation.2 | async-start | bytes 524288 | tf_op jit(solution)/shard_map/psum | solution.py:48
  149.6 103.4 %all-reduce.15.cloned.1.call-start = ((), (), s32[]{:S(2)}) async-start(), calls=%async_computation.3 | async-start | bytes 131072 | tf_op jit(solution)/shard_map/psum | solution.py:64
  200.7 101.7 %all-reduce.17.cloned.1.call-start = ((), (), s32[]{:S(2)}) async-start(), calls=%async_computation.4 | async-start | bytes 524288 | tf_op jit(solution)/shard_map/psum | solution.py:48
  270.1 103.4 %all-reduce.19.cloned.1.call-start = ((), (), s32[]{:S(2)}) async-start(), calls=%async_computation.5 | async-start | bytes 131072 | tf_op jit(solution)/shard_map/psum | solution.py:64
  321.1 101.7 %all-reduce.21.cloned.1.call-start = ((), (), s32[]{:S(2)}) async-start(), calls=%async_computation.6 | async-start | bytes 524288 | tf_op jit(solution)/shard_map/psum | solution.py:48
  390.5 103.5 %all-reduce.23.cloned.1.call-start = ((), (), s32[]{:S(2)}) async-start(), calls=%async_computation.7 | async-start | bytes 131072 | tf_op jit(solution)/shard_map/psum | solution.py:64
  422.8 84.5 %copy-start.1 = (f32[8,8192]{1,0:T(8,128)S(1)}, f32[8,8192]{1,0:T(8,128)}, u32[]{:S(2)}) copy-start(f32[8,8192]{1,0:T(8,128)} %all-reduce.21.cloned.1.call-done) | copy-start | bytes 786436
Sparse Core Ops, SparseCore 0:
  27.7 33.7 all-reduce.8
  80.4 52.1 all-reduce.10
  149.7 32.1 all-reduce.12
  200.8 52.1 all-reduce.14
  270.2 32.1 all-reduce.16
  321.3 52.1 all-reduce.18
  390.6 32.1 all-reduce.20
  441.7 52.1 all-reduce.22
where the time goes:
time: 516 us; the launch traced here: 515 us
  waiting for transfers between devices  340 us (66%)
  blocking collectives  108 us (21%)
  matrix products  29.3 us (6%)
  other arithmetic  17.7 us (3%)
  between operations  14.3 us (3%)
  local copies, waits for them, and re-layouts  5.99 us (1%)
    psum x4, waiting for transfers between devices, local(): summed = lax.psum(partial_value, 'cell')  209 us
    psum x4, waiting for transfers between devices, cols_reduce(): return lax.psum(adj_terms, 'ray')  131 us
    psum x5, blocking collectives, norm_rows(): total = lax.psum(local_sq, 'ray')  60.2 us
    psum x4, blocking collectives, norm_cols(): total = lax.psum(local_sq, 'cell')  47.3 us
    dot_general x4, matrix products, local(): jnp.einsum('bsrc,nbsc->nbr', tiles, picked, preferred_element_type=jnp.fl...  16.1 us
    dot_general x4, matrix products, adjoint(): jnp.einsum('bsrc,nbr->bsnc', tiles, rows, preferred_element_type=jnp.floa...  11.4 us
  transfers between devices with their start and end apart: 8, of which 8 were waited for; matrix products, arithmetic and copies ran while one was open for 0% of the time, Pallas kernels for 0%

commit v1 on v0

--- a/solution.py
+++ b/solution.py
@@ -61,7 +61,8 @@
             "bsrc,nbsc->nbr", tiles, picked, preferred_element_type=jnp.float32
         )
         partial_value = partial_value.reshape(nrhs, bundles * ray_rows)
-        summed = lax.psum(partial_value, "cell")
+        parts = lax.all_gather(partial_value, "cell", axis=0, tiled=False)
+        summed = parts.sum(axis=0)
         u_state = summed - alpha[:, None] * u_state
         beta = norm_rows(jnp.sum(u_state * u_state, axis=1))
         u_state = u_state / beta[:, None]

time: 516 us -> 337 us (0.65)
  waiting for transfers between devices: 340 us -> 132 us
  blocking collectives: 108 us -> 143 us
    psum x4 -> x0, waiting for transfers between devices: 209 us -> none  [local(): summed = lax.psum(partial_value, 'cell')]
    all_gather x0 -> x4, blocking collectives: none -> 39.4 us  [local(): parts = lax.all_gather(partial_value, 'cell', axis=0, tiled=False)]
  transfers between devices with their start and end apart: 8 -> 4, of which waited for: 8 -> 4; matrix products, arithmetic and copies ran while one was open for 0% -> 0% of each run, Pallas kernels for 0% -> 0%
where the time goes in v1:
time: 337 us; the launch traced here: 336 us
  blocking collectives  143 us (42%)
  waiting for transfers between devices  132 us (39%)
  matrix products  26.7 us (8%)
  other arithmetic  14.4 us (4%)
  between operations  13.9 us (4%)
  local copies, waits for them, and re-layouts  5.99 us (2%)
    psum x4, waiting for transfers between devices, cols_reduce(): return lax.psum(adj_terms, 'ray')  132 us
    psum x5, blocking collectives, norm_rows(): total = lax.psum(local_sq, 'ray')  56.1 us
    psum x4, blocking collectives, norm_cols(): total = lax.psum(local_sq, 'cell')  47.3 us
    all_gather x4, blocking collectives, local(): parts = lax.all_gather(partial_value, 'cell', axis=0, tiled=False)  39.4 us
    dot_general x4, matrix products, local(): jnp.einsum('bsrc,nbsc->nbr', tiles, picked, preferred_element_type=jnp.fl...  13.5 us
    dot_general x4, matrix products, adjoint(): jnp.einsum('bsrc,nbr->bsnc', tiles, rows, preferred_element_type=jnp.floa...  11.4 us
  transfers between devices with their start and end apart: 4, of which 4 were waited for; matrix products, arithmetic and copies ran while one was open for 0% of the time, Pallas kernels for 0%

profile of v1, /device:TPU:0, one launch (start us, length us, event | category | flops | bytes accessed | tf_op | source)
XLA Modules:
  0.0 336.2 jit_solution(2611223568040794773)
XLA Ops:
  7.2 0.0 all-reduce.5.cloned.1.call-start
  7.2 1.0 multiply_reduce_fusion.8
  8.2 13.5 %psum.91 = f32[8]{0:T(128)S(1)} all-reduce(f32[8]{0:T(128)S(1)} %multiply_reduce_fusion.8), channel_id=1, replica_groups=mesh['ray'=4,'cell'=8] {'ray'}, use_global_device_ids=true, to_apply=%region_1.0 | all-reduce | flops 8 | bytes 64 | tf_op jit(solution)/shard_map/psum | solution.py:11
  21.7 0.7 fusion.29
  22.4 0.1 copy.10
  22.5 0.9 fusion.23
  23.4 2.8 convolution_bitcast_fusion.7
  26.3 0.5 convolution_bitcast_fusion.3
  26.7 0.9 copy.28
  27.6 0.0 all-reduce.7.cloned.1.call-start
  27.7 0.1 copy.12
  27.8 0.1 reshape.111
  27.9 33.7 %all-reduce.5.cloned.1.call-done = f32[8,8192]{1,0:T(8,128)} async-done(((f32[8,8192]{1,0:T(8,128)}), f32[8,8192]{1,0:T(8,128)}) %all-reduce.5.cloned.1.call-update) | async-done | bytes 262160 | tf_op jit(solution)/shard_map/psum | solution.py:48
  61.6 1.1 multiply_reduce_fusion.3
  62.7 11.8 %psum.93 = f32[8]{0:T(128)S(1)} all-reduce(f32[8]{0:T(128)S(1)} %multiply_reduce_fusion.3), channel_id=1, replica_groups=mesh['ray'=4,'cell'=8] {'cell'}, use_global_device_ids=true, to_apply=%region_4.0 | all-reduce | flops 8 | bytes 64 | tf_op jit(solution)/shard_map/psum | solution.py:16
  74.5 1.0 fusion.38
  75.6 0.6 gather_fusion
  76.2 3.4 %fusion.10 = f32[8,8,256,1]{2,1,3,0:T(8,128)S(1)} fusion(bf16[8,4,256,256]{3,2,1,0:T(8,128)(2,1)} %param.5, bf16[8,4,8,256]{3,2,1,0:T(8,128)(2,1)S(1)} %bitcast.124, bf16[8,4]{1,0:T(8,128)(2,1)S(1)} %get-tuple-element.30), kind=kOutput, calls=%fused_computation.30 | convolution fusion | flops 33619968 | bytes 4390976 | tf_op jit(solution)/shard_map/bsrc,nbsc->nbr/dot_general | solution.py:60
  79.5 9.9 %all_gather.12 = f32[8,8,2048]{2,1,0:T(8,128)S(1)} all-gather(f32[1,8,2048]{2,1,0:T(8,128)S(1)} %bitcast.132), channel_id=1, replica_groups=mesh['ray'=4,'cell'=8] {'cell'}, dimensions={0}, use_global_device_ids=true | all-gather | bytes 589824 | tf_op jit(solution)/shard_map/all_gather | solution.py:64
  89.5 0.2 multiply_reduce_fusion.7
  89.7 10.7 %psum.94 = f32[8]{0:T(128)S(1)} all-reduce(f32[8]{0:T(128)S(1)} %get-tuple-element.21), channel_id=1, replica_groups=mesh['ray'=4,'cell'=8] {'ray'}, use_global_device_ids=true, to_apply=%region_7.0 | all-reduce | flops 8 | bytes 64 | tf_op jit(solution)/shard_map/psum | solution.py:11
  100.4 0.1 fusion.24
  100.5 2.9 convolution_bitcast_fusion.6
  103.3 0.5 convolution_bitcast_fusion.2
  103.8 0.9 copy.29
  104.7 0.0 all-reduce.9.cloned.1.call-start
  104.7 32.7 %all-reduce.7.cloned.1.call-done = f32[8,8192]{1,0:T(8,128)} async-done(((f32[8,8192]{1,0:T(8,128)}), f32[8,8192]{1,0:T(8,128)}) %all-reduce.7.cloned.1.call-update) | async-done | bytes 262160 | tf_op jit(solution)/shard_map/psum | solution.py:48
  137.5 1.2 multiply_reduce_fusion.2
  138.7 11.8 %psum.96 = f32[8]{0:T(128)S(1)} all-reduce(f32[8]{0:T(128)S(1)} %multiply_reduce_fusion.2), channel_id=1, replica_groups=mesh['ray'=4,'cell'=8] {'cell'}, use_global_device_ids=true, to_apply=%region_10.0 | all-reduce | flops 8 | bytes 64 | tf_op jit(solution)/shard_map/psum | solution.py:16
  150.5 1.1 fusion.46
  151.6 0.6 gather_fusion.1
  152.2 3.4 %fusion.8 = f32[8,8,256,1]{2,1,3,0:T(8,128)S(1)} fusion(bf16[8,4,256,256]{3,2,1,0:T(8,128)(2,1)} %param.5, bf16[8,4,8,256]{3,2,1,0:T(8,128)(2,1)S(1)} %bitcast.125, bf16[8,4]{1,0:T(8,128)(2,1)S(1)} %get-tuple-element.30), kind=kOutput, calls=%fused_computation.28 | convolution fusion | flops 33619968 | bytes 4390976 | tf_op jit(solution)/shard_map/bsrc,nbsc->nbr/dot_general | solution.py:60
  155.5 9.8 %all_gather.13 = f32[8,8,2048]{2,1,0:T(8,128)S(1)} all-gather(f32[1,8,2048]{2,1,0:T(8,128)S(1)} %bitcast.133), channel_id=1, replica_groups=mesh['ray'=4,'cell'=8] {'cell'}, dimensions={0}, use_global_device_ids=true | all-gather | bytes 589824 | tf_op jit(solution)/shard_map/all_gather | solution.py:64
  165.4 0.2 multiply_reduce_fusion.6
  165.6 10.7 %psum.97 = f32[8]{0:T(128)S(1)} all-reduce(f32[8]{0:T(128)S(1)} %get-tuple-element.17), channel_id=1, replica_groups=mesh['ray'=4,'cell'=8] {'ray'}, use_global_device_ids=true, to_apply=%region_13.0 | all-reduce | flops 8 | bytes 64 | tf_op jit(solution)/shard_map/psum | solution.py:11
  176.2 0.1 fusion.25
  176.3 2.9 convolution_bitcast_fusion.5
  179.2 0.5 convolution_bitcast_fusion.1
  179.6 0.9 copy.30
  180.5 0.0 all-reduce.11.cloned.1.call-start
  180.6 32.7 %all-reduce.9.cloned.1.call-done = f32[8,8192]{1,0:T(8,128)} async-done(((f32[8,8192]{1,0:T(8,128)}), f32[8,8192]{1,0:T(8,128)}) %all-reduce.9.cloned.1.call-update) | async-done | bytes 262160 | tf_op jit(solution)/shard_map/psum | solution.py:48
  213.3 1.2 multiply_reduce_fusion.1
  214.5 11.8 %psum.99 = f32[8]{0:T(128)S(1)} all-reduce(f32[8]{0:T(128)S(1)} %multiply_reduce_fusion.1), channel_id=1, replica_groups=mesh['ray'=4,'cell'=8] {'cell'}, use_global_device_ids=true, to_apply=%region_16.0 | all-reduce | flops 8 | bytes 64 | tf_op jit(solution)/shard_map/psum | solution.py:16
  226.3 1.1 fusion.45
  227.4 0.6 gather_fusion.2
  228.0 3.4 %fusion.6 = f32[8,8,256,1]{2,1,3,0:T(8,128)S(1)} fusion(bf16[8,4,256,256]{3,2,1,0:T(8,128)(2,1)} %param.5, bf16[8,4,8,256]{3,2,1,0:T(8,128)(2,1)S(1)} %bitcast.126, bf16[8,4]{1,0:T(8,128)(2,1)S(1)} %get-tuple-element.30), kind=kOutput, calls=%fused_computation.26 | convolution fusion | flops 33619968 | bytes 4390976 | tf_op jit(solution)/shard_map/bsrc,nbsc->nbr/dot_general | solution.py:60
  231.4 9.8 %all_gather.14 = f32[8,8,2048]{2,1,0:T(8,128)S(1)} all-gather(f32[1,8,2048]{2,1,0:T(8,128)S(1)} %bitcast.134), channel_id=1, replica_groups=mesh['ray'=4,'cell'=8] {'cell'}, dimensions={0}, use_global_device_ids=true | all-gather | bytes 589824 | tf_op jit(solution)/shard_map/all_gather | solution.py:64
  241.2 0.2 multiply_reduce_fusion.5
  241.4 10.7 %psum.100 = f32[8]{0:T(128)S(1)} all-reduce(f32[8]{0:T(128)S(1)} %get-tuple-element.13), channel_id=1, replica_groups=mesh['ray'=4,'cell'=8] {'ray'}, use_global_device_ids=true, to_apply=%region_19.0 | all-reduce | flops 8 | bytes 64 | tf_op jit(solution)/shard_map/psum | solution.py:11
  252.1 0.1 fusion.26
  252.1 2.9 convolution_bitcast_fusion.4
  255.0 0.5 convolution_bitcast_fusion
  255.5 0.9 copy.31
  256.4 33.0 %all-reduce.11.cloned.1.call-done = f32[8,8192]{1,0:T(8,128)} async-done(((f32[8,8192]{1,0:T(8,128)}), f32[8,8192]{1,0:T(8,128)}) %all-reduce.11.cloned.1.call-update) | async-done | bytes 262160 | tf_op jit(solution)/shard_map/psum | solution.py:48
  289.3 1.3 multiply_reduce_fusion
  290.6 11.8 %psum.102 = f32[8]{0:T(128)S(1)} all-reduce(f32[8]{0:T(128)S(1)} %multiply_reduce_fusion), channel_id=1, replica_groups=mesh['ray'=4,'cell'=8] {'cell'}, use_global_device_ids=true, to_apply=%region_22.0 | all-reduce | flops 8 | bytes 64 | tf_op jit(solution)/shard_map/psum | solution.py:16
  302.4 1.1 fusion.20
  303.5 0.6 gather_fusion.3
  304.1 3.4 %fusion.4 = f32[8,8,256,1]{2,1,3,0:T(8,128)S(1)} fusion(bf16[8,4,256,256]{3,2,1,0:T(8,128)(2,1)} %param.5, bf16[8,4,8,256]{3,2,1,0:T(8,128)(2,1)S(1)} %bitcast.123, bf16[8,4]{1,0:T(8,128)(2,1)S(1)} %get-tuple-element.30), kind=kOutput, calls=%fused_computation.24 | convolution fusion | flops 33619968 | bytes 4390976 | tf_op jit(solution)/shard_map/bsrc,nbsc->nbr/dot_general | solution.py:60
  307.4 9.8 %all_gather.15 = f32[8,8,2048]{2,1,0:T(8,128)S(1)} all-gather(f32[1,8,2048]{2,1,0:T(8,128)S(1)} %bitcast.131), channel_id=1, replica_groups=mesh['ray'=4,'cell'=8] {'cell'}, dimensions={0}, use_global_device_ids=true | all-gather | bytes 589824 | tf_op jit(solution)/shard_map/all_gather | solution.py:64
  317.3 0.2 multiply_reduce_fusion.4
  317.5 10.7 %psum.103 = f32[8]{0:T(128)S(1)} all-reduce(f32[8]{0:T(128)S(1)} %multiply_reduce_fusion.4), channel_id=1, replica_groups=mesh['ray'=4,'cell'=8] {'ray'}, use_global_device_ids=true, to_apply=%region_25.0 | all-reduce | flops 8 | bytes 64 | tf_op jit(solution)/shard_map/psum | solution.py:11
  328.1 0.6 divide_multiply_fusion
  328.8 0.9 multiply_add_fusion
  (27 shorter events, 0.3 us)
Async XLA Ops:
  7.2 19.1 %copy-start.3 = (s32[8,4]{0,1:T(4,128)S(1)}, s32[8,4]{0,1:T(4,128)}, u32[]{:S(2)}) copy-start(s32[8,4]{0,1:T(4,128)} %param.6) | copy-start | bytes 388
  7.2 54.4 %all-reduce.5.cloned.1.call-start = ((), (), s32[]{:S(2)}) async-start(), calls=%async_computation | async-start | bytes 524288 | tf_op jit(solution)/shard_map/psum | solution.py:48
  26.3 63.3 %copy-start.2 = (f32[8,2048]{1,0:T(8,128)S(1)}, f32[8,2048]{1,0:T(8,128)}, u32[]{:S(2)}) copy-start(f32[8,2048]{1,0:T(8,128)} %param.4) | copy-start | bytes 196612
  27.6 109.8 %all-reduce.7.cloned.1.call-start = ((), (), s32[]{:S(2)}) async-start(), calls=%async_computation.1 | async-start | bytes 524288 | tf_op jit(solution)/shard_map/psum | solution.py:48
  79.5 57.9 %copy-start = (f32[8,8192]{1,0:T(8,128)S(1)}, f32[8,8192]{1,0:T(8,128)}, u32[]{:S(2)}) copy-start(f32[8,8192]{1,0:T(8,128)} %all-reduce.5.cloned.1.call-done) | copy-start | bytes 786436
  104.7 108.6 %all-reduce.9.cloned.1.call-start = ((), (), s32[]{:S(2)}) async-start(), calls=%async_computation.2 | async-start | bytes 524288 | tf_op jit(solution)/shard_map/psum | solution.py:48
  180.5 108.8 %all-reduce.11.cloned.1.call-start = ((), (), s32[]{:S(2)}) async-start(), calls=%async_computation.3 | async-start | bytes 524288 | tf_op jit(solution)/shard_map/psum | solution.py:48
  289.3 39.4 %copy-start.1 = (f32[8,8192]{1,0:T(8,128)S(1)}, f32[8,8192]{1,0:T(8,128)}, u32[]{:S(2)}) copy-start(f32[8,8192]{1,0:T(8,128)} %all-reduce.11.cloned.1.call-done) | copy-start | bytes 786436
Sparse Core Ops, SparseCore 0:
  27.7 33.7 all-reduce.4
  104.8 32.6 all-reduce.6
  180.6 32.6 all-reduce.8
  256.5 32.7 all-reduce.10
